TPU v7x, 32 devices: a whole 2x2x4 slice. The times are simulated.
32 devices in a mesh: rows: 4 (over x, core), cols: 8 (over z, y).
Axes of the slice: x: 2, y: 2, z: 4, core: 2. Of those that a mesh axis runs over, the one named last changes fastest.
Arguments:
- tensor: float32 [48, 256, 512], P('rows', 'cols'), may hold values from 0 to 1
- first_factor: float32 [48, 256], P('rows', 'cols'), may hold values from -2.5 to 2.5
- second_factor: float32 [256, 256], P('cols', 'rows'), may hold values from -2.5 to 2.5
- third_factor: float32 [512, 256], P(('rows', 'cols')), may hold values from -2.5 to 2.5
Outputs:
- first_new: float32 [48, 256], P('rows', 'cols')
- second_new: float32 [256, 256], P('cols', 'rows')
- third_new: float32 [512, 256], P(('rows', 'cols'))
All inputs are finite; a program needn't handle non-finite values.
Results may differ from a plain program's by a relative error of at most 0.0003.
Values sent between devices are 32-bit elements; how exact they have to be, the bound alone decides.
A program may use at most 64 MiB of HBM per device.

v0:
```python
import functools

import jax
import jax.numpy as jnp
from jax import lax
from jax.experimental import pallas as pl
from jax.experimental.pallas import tpu as pltpu
from jax.sharding import PartitionSpec as P

STEPS = 2
MESH = pl.DeviceIdType.MESH


def gather_third(piece):
    return lax.all_gather(piece, ("rows", "cols"), axis=0, tiled=True)


def plain_steps(tensor, first_factor, second_factor, third_factor):
    high = lax.Precision.HIGHEST
    rows_dev, cols_dev, depth = tensor.shape
    rate_a, rate_b, rate_c = rates(tensor)
    flat_target = tensor.reshape(-1, depth)
    shard_a, shard_b = (first_factor, second_factor)
    whole_c = gather_third(third_factor)
    for step_index in range(STEPS):
        whole_a = lax.all_gather(shard_a, "cols", axis=1, tiled=True)
        whole_b = lax.all_gather(shard_b, "rows", axis=1, tiled=True)
        khatri = (whole_a[:, None, :] * whole_b[None, :, :]).reshape(-1, whole_a.shape[1])
        model_tile = jnp.dot(khatri, whole_c.T, precision=high, preferred_element_type=jnp.float32)
        deriv = jax.nn.sigmoid(model_tile) - flat_target
        deriv_c = jnp.dot(
            deriv, whole_c, precision=high, preferred_element_type=jnp.float32
        ).reshape(rows_dev, cols_dev, -1)
        term_a = jnp.einsum("ijr,jr->ir", deriv_c, whole_b, precision=high)
        term_b = jnp.einsum("ijr,ir->jr", deriv_c, whole_a, precision=high)
        term_c = lax.dot_general(
            deriv, khatri, (((0,), (0,)), ((), ())), precision=high,
            preferred_element_type=jnp.float32,
        )
        shard_a = shard_a - rate_a * lax.psum_scatter(
            term_a, "cols", scatter_dimension=1, tiled=True
        )
        shard_b = shard_b - rate_b * lax.psum_scatter(
            term_b, "rows", scatter_dimension=1, tiled=True
        )
        whole_c = whole_c - rate_c * lax.psum(term_c, ("rows", "cols"))
    owner = lax.axis_index("rows") * lax.axis_size("cols") + lax.axis_index("cols")
    count = third_factor.shape[0]
    shard_c = lax.dynamic_slice_in_dim(whole_c, owner * count, count, 0)
    return (shard_a, shard_b, shard_c)


def rates(tensor):
    rows_dev, cols_dev, depth = tensor.shape
    size_i = rows_dev * lax.axis_size("rows")
    size_j = cols_dev * lax.axis_size("cols")
    return (
        4.0 / float(size_j * depth) ** 0.5,
        4.0 / float(size_i * depth) ** 0.5,
        4.0 / float(size_i * size_j) ** 0.5,
    )


def split(x):
    hi = x.astype(jnp.bfloat16)
    return hi, (x - hi.astype(jnp.float32)).astype(jnp.bfloat16)


def dot3(lhs, rhs, dims):
    def one(a, b):
        return lax.dot_general(a, b, (dims, ((), ())), preferred_element_type=jnp.float32)

    return one(lhs[0], rhs[0]) + (one(lhs[0], rhs[1]) + one(lhs[1], rhs[0]))


def kernel(
    n_rows, n_cols, rate, target_ref, a_ref, b_ref, c_ref, a_out, b_out, c_out,
    target, a_slots, a_rows, a_leave, a_arrive, b_slots, c_whole, c_leave, c_arrive,
    khatri_hi, khatri_lo, prob, place_a, place_b, own_sem, send_sem, recv_sem,
):
    half = n_rows // 2
    n_i, n_j = a_ref.shape[0], b_ref.shape[0]
    width_a, width_b = a_ref.shape[1], b_ref.shape[1]
    rank = c_ref.shape[1]
    depth = target.shape[2]
    row, col = lax.axis_index("rows"), lax.axis_index("cols")
    plane, core = lax.div(row, 2), lax.rem(row, 2)
    used = []

    def turn(base, offset, size):
        return lax.rem(base + offset, size)

    def send(src, dst, to_row, to_col):
        number = len(used)
        copy = pltpu.make_async_remote_copy(
            src_ref=src, dst_ref=dst, send_sem=send_sem.at[number], recv_sem=recv_sem.at[number],
            device_id=(to_row, to_col), device_id_type=MESH,
        )
        used.append(copy)
        copy.start()
        return copy

    steps_away = [(h, flip) for h in range(half) for flip in (0, 1)][1:]
    to_rows = [turn(plane, h, half) * 2 + lax.rem(core + flip, 2) for h, flip in steps_away]
    of_rows = [turn(plane, half - h, half) * 2 + lax.rem(core + flip, 2) for h, flip in steps_away]
    to_cols = [turn(col, k, n_cols) for k in range(1, n_cols)]

    own = pltpu.make_async_copy(
        target_ref.at[:, pl.ds(pl.multiple_of(row * depth, 128), depth)], target.at[row], own_sem.at[0]
    )
    own.start()
    barrier = pltpu.get_barrier_semaphore()
    for there in to_cols:
        pl.semaphore_signal(barrier, inc=1, device_id=(row, there), device_id_type=MESH)
    for there in to_rows:
        pl.semaphore_signal(barrier, inc=1, device_id=(there, col), device_id_type=MESH)
    pl.semaphore_wait(barrier, n_cols + n_rows - 2)

    def over_cols(src, dst):
        return [send(src, dst, row, there) for there in to_cols]

    def over_rows(src, dst):
        return [send(src, dst, there, col) for there in to_rows]

    def arrived(copies):
        for copy in copies:
            copy.wait_recv()

    def total(slots, version):
        result = slots[version, 0]
        for k in range(1, slots.shape[1]):
            result = result + slots[version, k]
        return result

    def share(slots, version, place, spread):
        return spread(slots.at[version, place], slots.at[version, place])

    sent_c = over_cols(c_ref, c_whole.at[0, col])
    place_a[...] = jnp.zeros_like(place_a)
    place_a[:n_i, :width_a] = a_ref[...]
    a_slots[0, col] = pltpu.roll(place_a[...], col * width_a, 1)
    sent_a = share(a_slots, 0, col, over_cols)
    place_b[...] = jnp.zeros_like(place_b)
    place_b[:, :width_b] = b_ref[...]
    b_slots[0, row] = pltpu.roll(place_b[...], row * width_b, 1)
    sent_b = share(b_slots, 0, row, over_rows)
    sent_target = [
        send(
            target_ref.at[:, pl.ds(pl.multiple_of(there * depth, 128), depth)],
            target.at[row], there, col,
        )
        for there in to_rows
    ]
    c_shard = c_ref[...]
    c_whole[0, col] = c_shard
    arrived(sent_a)
    a_own = total(a_slots, 0)
    a_rows[0, row] = a_own
    sent_rows = share(a_rows, 0, row, over_rows)
    arrived(sent_b)
    b_full = total(b_slots, 0)

    for step in range(STEPS):
        last = step == STEPS - 1
        blocks = [row] + of_rows
        for number, block in enumerate(blocks):
            if number:
                sent_rows[number - 1].wait_recv()
            a_block = a_rows[step, block]
            for i in range(n_i):
                hi, lo = split(a_block[i : i + 1, :] * b_full)
                khatri_hi[block, i * n_j : (i + 1) * n_j, :] = hi
                khatri_lo[block, i * n_j : (i + 1) * n_j, :] = lo
            if not number:
                arrived(sent_c)
                c_parts = split(c_whole[step].reshape(-1, rank))
            model = dot3((khatri_hi[block], khatri_lo[block]), c_parts, ((1,), (1,)))
            prob[block] = jax.nn.sigmoid(model)
        order = list(range(n_rows)) if step == 0 else list(range(1, n_rows)) + [0]
        term_c, term_b, term_own = None, None, None
        sent_terms = [None] * (n_rows - 1)
        derivs = {}
        for number in order:
            block = blocks[number]
            if step == 0:
                if number:
                    sent_target[number - 1].wait_recv()
                else:
                    own.wait()
            derivs[number] = split(prob[block] - target[block])
            part_c = dot3(derivs[number], (khatri_hi[block], khatri_lo[block]), ((0,), (0,)))
            term_c = part_c if term_c is None else term_c + part_c
        c_leave[step] = term_c.reshape(c_leave.shape[1:])
        sent_c = [
            send(c_leave.at[step, there], c_arrive.at[step, k], row, there)
            for k, there in enumerate(to_cols)
        ]
        for number in list(range(1, n_rows)) + [0]:
            block = blocks[number]
            deriv_c = dot3(derivs[number], c_parts, ((1,), (0,))).reshape(n_i, n_j, rank)
            term_a = jnp.sum(deriv_c * b_full[None, :, :], axis=1)
            if number:
                a_leave[step, number - 1] = jnp.zeros_like(place_a)
                a_leave[step, number - 1, :n_i, :] = term_a
                sent_terms[number - 1] = send(
                    a_leave.at[step, number - 1], a_arrive.at[step, number - 1], block, col
                )
            else:
                term_own = term_a
            a_block = a_rows[step, block][:n_i, :]
            part_b = jnp.sum(deriv_c * a_block[:, None, :], axis=0)
            term_b = part_b if term_b is None else term_b + part_b
        b_slots[step + 1, row] = term_b
        sent_b = share(b_slots, step + 1, row, over_rows)
        place_a[...] = jnp.zeros_like(place_a)
        place_a[:n_i, :] = term_own
        arrived(sent_terms)
        term_own = place_a[...]
        for k in range(n_rows - 1):
            term_own = term_own + a_arrive[step, k]
        a_slots[step + 1, col] = term_own
        sent_a = share(a_slots, step + 1, col, over_cols)
        arrived(sent_c)
        grad_c = c_leave[step, col]
        for k in range(n_cols - 1):
            grad_c = grad_c + c_arrive[step, k]
        c_shard = c_shard - rate[2] * grad_c
        if last:
            c_out[...] = c_shard
        else:
            c_whole[step + 1, col] = c_shard
            sent_c = share(c_whole, step + 1, col, over_cols)
        arrived(sent_a)
        a_own = a_own - rate[0] * total(a_slots, step + 1)
        if not last:
            a_rows[step + 1, row] = a_own
            sent_rows = share(a_rows, step + 1, row, over_rows)
        arrived(sent_b)
        b_full = b_full - rate[1] * total(b_slots, step + 1)
    back = lax.rem(n_cols - col, n_cols) * width_a
    a_out[...] = pltpu.roll(a_own, back, 1)[:n_i, :width_a]
    back = lax.rem(n_rows - row, n_rows) * width_b
    b_out[...] = pltpu.roll(b_full, back, 1)[:, :width_b]
    for copy in used:
        copy.wait_send()


def n_copies(n_rows, n_cols):
    rows, cols = n_rows - 1, n_cols - 1
    return rows + (STEPS + 1) * (cols + rows) + STEPS * (rows + cols) + STEPS * (rows + cols)


def per_device(tensor, first_factor, second_factor, third_factor):
    n_rows, n_cols = lax.axis_size("rows"), lax.axis_size("cols")
    count, rank = third_factor.shape
    n_i, n_j, depth = tensor.shape
    part = depth // n_rows
    if count % 8 or n_rows % 2 or n_j % 16 or part % 128:
        return plain_steps(tensor, first_factor, second_factor, third_factor)
    tall = -(-n_i // 8) * 8
    f32, bf16 = jnp.float32, jnp.bfloat16
    copies = n_copies(n_rows, n_cols)
    vmem = pl.BlockSpec(memory_space=pltpu.VMEM)
    return pl.pallas_call(
        functools.partial(kernel, n_rows, n_cols, rates(tensor)),
        out_shape=tuple(
            jax.ShapeDtypeStruct(x.shape, f32) for x in (first_factor, second_factor, third_factor)
        ),
        in_specs=[pl.BlockSpec(memory_space=pltpu.HBM)] + [vmem] * 3,
        out_specs=(vmem,) * 3,
        scratch_shapes=[
            pltpu.VMEM((n_rows, n_i * n_j, part), f32),
            pltpu.VMEM((STEPS + 1, n_cols, tall, rank), f32),
            pltpu.VMEM((STEPS, n_rows, tall, rank), f32),
            pltpu.VMEM((STEPS, n_rows - 1, tall, rank), f32),
            pltpu.VMEM((STEPS, n_rows - 1, tall, rank), f32),
            pltpu.VMEM((STEPS + 1, n_rows, n_j, rank), f32),
            pltpu.VMEM((STEPS, n_cols, count, rank), f32),
            pltpu.VMEM((STEPS, n_cols, count, rank), f32),
            pltpu.VMEM((STEPS, n_cols - 1, count, rank), f32),
            pltpu.VMEM((n_rows, n_i * n_j, rank), bf16),
            pltpu.VMEM((n_rows, n_i * n_j, rank), bf16),
            pltpu.VMEM((n_rows, n_i * n_j, part), f32),
            pltpu.VMEM((tall, rank), f32),
            pltpu.VMEM((n_j, rank), f32),
            pltpu.SemaphoreType.DMA((1,)),
            pltpu.SemaphoreType.DMA((copies,)),
            pltpu.SemaphoreType.DMA((copies,)),
        ],
        compiler_params=pltpu.CompilerParams(
            collective_id=0, has_side_effects=True, vmem_limit_bytes=48 << 20
        ),
    )(tensor.reshape(n_i * n_j, depth), first_factor, second_factor, third_factor)


def solution(mesh):
    in_specs = (
        P("rows", "cols", None),
        P("rows", "cols"),
        P("cols", "rows"),
        P(("rows", "cols"), None),
    )
    out_specs = (P("rows", "cols"), P("cols", "rows"), P(("rows", "cols"), None))
    return jax.shard_map(
        per_device, mesh=mesh, in_specs=in_specs, out_specs=out_specs, check_vma=False
    )
```

profile of v0, /device:TPU:0, one launch (start us, length us, event | category | flops | bytes accessed | tf_op | source)
XLA Modules:
  0.0 49.3 jit_solution(5897068548290422773)
XLA Ops:
  0.6 0.0 copy-start
  0.6 1.1 %copy-done = f32[12,32,512]{2,1,0:T(8,128)S(1)} copy-done((f32[12,32,512]{2,1,0:T(8,128)S(1)}, f32[12,32,512]{2,1,0:T(8,128)}, u32[]{:S(2)}) %copy-start) | copy-done | bytes 786456
  1.8 0.0 copy-start.1
  1.8 0.7 %copy-done.1 = f32[32,64]{1,0:T(8,128)S(1)} copy-done((f32[32,64]{1,0:T(8,128)S(1)}, f32[32,64]{1,0:T(8,128)}, u32[]{:S(2)}) %copy-start.1) | copy-done | bytes 8216
  2.5 0.0 copy-start.2
  2.5 0.7 %copy-done.2 = f32[16,256]{1,0:T(8,128)S(1)} copy-done((f32[16,256]{1,0:T(8,128)S(1)}, f32[16,256]{1,0:T(8,128)}, u32[]{:S(2)}) %copy-start.2) | copy-done | bytes 16408
  3.2 0.0 copy-start.3
  3.2 0.7 %copy-done.3 = f32[12,32]{1,0:T(8,128)S(1)} copy-done((f32[12,32]{1,0:T(8,128)S(1)}, f32[12,32]{1,0:T(8,128)}, u32[]{:S(2)}) %copy-start.3) | copy-done | bytes 1560
  3.9 43.6 %shard_map.67 = (f32[12,32]{1,0:T(8,128)S(1)}, f32[32,64]{1,0:T(8,128)S(1)}, f32[16,256]{1,0:T(8,128)S(1)}) custom-call(f32[384,512]{1,0:T(8,128)S(1)} %bitcast.1, f32[12,32]{1,0:T(8,128)S(1)} %copy-done.3, f32[32,64]{1,0:T(8,128)S(1)} %copy-done.1, f32[16,256]{1,0:T(8,128)S(1)} %copy-done.2), custom_call_target="tpu_custom_call" | custom-call | tf_op jit(solution)/shard_map/pallas_call | solution.py:264
  47.5 0.6 %copy.10 = f32[12,32]{1,0:T(8,128)} copy(f32[12,32]{1,0:T(8,128)S(1)} %get-tuple-element.6) | data formatting | bytes 3072
  48.1 0.6 %copy.11 = f32[32,64]{1,0:T(8,128)} copy(f32[32,64]{1,0:T(8,128)S(1)} %get-tuple-element.7) | data formatting | bytes 16384
  48.7 0.6 %copy.12 = f32[16,256]{1,0:T(8,128)} copy(f32[16,256]{1,0:T(8,128)S(1)} %get-tuple-element.8) | data formatting | bytes 32768
Async XLA Ops:
  0.6 1.1 %copy-start = (f32[12,32,512]{2,1,0:T(8,128)S(1)}, f32[12,32,512]{2,1,0:T(8,128)}, u32[]{:S(2)}) copy-start(f32[12,32,512]{2,1,0:T(8,128)} %param.4) | copy-start | bytes 2359300
  1.8 0.7 %copy-start.1 = (f32[32,64]{1,0:T(8,128)S(1)}, f32[32,64]{1,0:T(8,128)}, u32[]{:S(2)}) copy-start(f32[32,64]{1,0:T(8,128)} %b_ref.1) | copy-start | bytes 24580
  2.5 0.7 %copy-start.2 = (f32[16,256]{1,0:T(8,128)S(1)}, f32[16,256]{1,0:T(8,128)}, u32[]{:S(2)}) copy-start(f32[16,256]{1,0:T(8,128)} %c_ref.1) | copy-start | bytes 49156
  3.2 0.7 %copy-start.3 = (f32[12,32]{1,0:T(8,128)S(1)}, f32[12,32]{1,0:T(8,128)}, u32[]{:S(2)}) copy-start(f32[12,32]{1,0:T(8,128)} %a_ref.1) | copy-start | bytes 4612
where the time goes:
time: 49.7 us; the launch traced here: 49.3 us
  Pallas kernels  43.6 us (88%)
  local copies, waits for them, and re-layouts  5.07 us (10%)
  between operations  0.65 us (1%)
    pallas_call x1, Pallas kernels, per_device(): pl.pallas_call(functools.partial(kernel, n_rows, n_cols, rates(tensor)),...  43.6 us
    unnamed x11, local copies, waits for them, and re-layouts  5.07 us

commit v1 on v0

v1 whole, which is shorter than its diff:
```python
import functools

import jax
import jax.numpy as jnp
from jax import lax
from jax.experimental import pallas as pl
from jax.experimental.pallas import tpu as pltpu
from jax.sharding import PartitionSpec as P

STEPS = 2
VMEM_LIMIT = 67043328
MESH = pl.DeviceIdType.MESH


def gather_third(piece):
    return lax.all_gather(piece, ("rows", "cols"), axis=0, tiled=True)


def plain_steps(tensor, first_factor, second_factor, third_factor):
    high = lax.Precision.HIGHEST
    rows_dev, cols_dev, depth = tensor.shape
    rate_a, rate_b, rate_c = rates(tensor)
    flat_target = tensor.reshape(-1, depth)
    shard_a, shard_b = (first_factor, second_factor)
    whole_c = gather_third(third_factor)
    for step_index in range(STEPS):
        whole_a = lax.all_gather(shard_a, "cols", axis=1, tiled=True)
        whole_b = lax.all_gather(shard_b, "rows", axis=1, tiled=True)
        khatri = (whole_a[:, None, :] * whole_b[None, :, :]).reshape(-1, whole_a.shape[1])
        model_tile = jnp.dot(khatri, whole_c.T, precision=high, preferred_element_type=jnp.float32)
        deriv = jax.nn.sigmoid(model_tile) - flat_target
        deriv_c = jnp.dot(
            deriv, whole_c, precision=high, preferred_element_type=jnp.float32
        ).reshape(rows_dev, cols_dev, -1)
        term_a = jnp.einsum("ijr,jr->ir", deriv_c, whole_b, precision=high)
        term_b = jnp.einsum("ijr,ir->jr", deriv_c, whole_a, precision=high)
        term_c = lax.dot_general(
            deriv, khatri, (((0,), (0,)), ((), ())), precision=high,
            preferred_element_type=jnp.float32,
        )
        shard_a = shard_a - rate_a * lax.psum_scatter(
            term_a, "cols", scatter_dimension=1, tiled=True
        )
        shard_b = shard_b - rate_b * lax.psum_scatter(
            term_b, "rows", scatter_dimension=1, tiled=True
        )
        whole_c = whole_c - rate_c * lax.psum(term_c, ("rows", "cols"))
    owner = lax.axis_index("rows") * lax.axis_size("cols") + lax.axis_index("cols")
    count = third_factor.shape[0]
    shard_c = lax.dynamic_slice_in_dim(whole_c, owner * count, count, 0)
    return (shard_a, shard_b, shard_c)


def rates(tensor):
    rows_dev, cols_dev, depth = tensor.shape
    size_i = rows_dev * lax.axis_size("rows")
    size_j = cols_dev * lax.axis_size("cols")
    return (
        4.0 / float(size_j * depth) ** 0.5,
        4.0 / float(size_i * depth) ** 0.5,
        4.0 / float(size_i * size_j) ** 0.5,
    )


def split(x):
    hi = x.astype(jnp.bfloat16)
    return hi, (x - hi.astype(jnp.float32)).astype(jnp.bfloat16)


def dot(lhs, rhs, dims):
    return lax.dot_general(lhs, rhs, (dims, ((), ())), preferred_element_type=jnp.float32)


def kernel(
    n_rows, n_cols, rate, target_hbm, a_hbm, b_hbm, c_hbm, a_out, b_out, c_out,
    stage, target, a_in, b_in, a_parts, b_parts, a_slots, a_rows, a_leave, a_arrive, b_slots,
    c_whole, c_leave, c_arrive, khatri_hi, khatri_lo, deriv, place_a, place_b,
    own_sem, ok_sem, send_sem, recv_sem,
):
    half = n_rows // 2
    n_i, n_j = a_in.shape[0], b_in.shape[0]
    width_a, width_b = a_in.shape[1], b_in.shape[1]
    rank = c_hbm.shape[1]
    depth = target.shape[2]
    row, col = lax.axis_index("rows"), lax.axis_index("cols")
    plane, core = lax.div(row, 2), lax.rem(row, 2)
    used, loads = [], []

    def turn(base, offset, size):
        return lax.rem(base + offset, size)

    def load(src, dst):
        copy = pltpu.make_async_copy(src, dst, own_sem.at[len(loads)])
        loads.append(copy)
        copy.start()
        return copy

    def send(src, dst, to_row, to_col):
        number = len(used)
        copy = pltpu.make_async_remote_copy(
            src_ref=src, dst_ref=dst, send_sem=send_sem.at[number], recv_sem=recv_sem.at[number],
            device_id=(to_row, to_col), device_id_type=MESH,
        )
        used.append(copy)
        copy.start()
        return copy

    steps_away = [(h, flip) for h in range(half) for flip in (0, 1)][1:]
    to_rows = [turn(plane, h, half) * 2 + lax.rem(core + flip, 2) for h, flip in steps_away]
    of_rows = [turn(plane, half - h, half) * 2 + lax.rem(core + flip, 2) for h, flip in steps_away]
    to_cols = [turn(col, k, n_cols) for k in range(1, n_cols)]

    def lanes(block):
        return pl.ds(pl.multiple_of(block * depth, 128), depth)

    def greet(there_row, there_col):
        pl.semaphore_signal(
            barrier, inc=1, device_id=(there_row, there_col), device_id_type=MESH
        )

    barrier = pltpu.get_barrier_semaphore()
    for h in range(1, half):
        greet(turn(plane, h, half) * 2, col)

    @pl.when(core == 1)
    def _():
        greet(row - 1, col)

    for there in to_cols:
        greet(plane * 2 + 1, there)

    got_b = load(b_hbm, b_in)
    got_target = load(target_hbm, stage)
    got_a = load(a_hbm, a_in)
    got_c = load(c_hbm, c_whole.at[0, col])
    got_own = load(target_hbm.at[:, lanes(row)], target.at[row])

    def over_cols(src, dst):
        return [send(src, dst, row, there) for there in to_cols]

    def over_rows(src, dst):
        return [send(src, dst, there, col) for there in to_rows]

    def arrived(copies):
        for copy in copies:
            copy.wait_recv()

    def total(slots, version):
        result = slots[version, 0]
        for k in range(1, slots.shape[1]):
            result = result + slots[version, k]
        return result

    def share(slots, version, place, spread):
        return spread(slots.at[version, place], slots.at[version, place])

    def widen(parts, width):
        per = 128 // width
        pieces = []
        for first in range(0, parts.shape[0], per):
            piece = parts[first]
            for k in range(1, per):
                piece = piece + parts[first + k]
            pieces.append(piece)
        return jnp.concatenate(pieces, axis=1)

    got_b.wait()
    place_b[...] = jnp.zeros_like(place_b)
    place_b[:, :width_b] = b_in[...]
    b_parts[row] = pltpu.roll(place_b[...], lax.rem(row, 128 // width_b) * width_b, 1)
    got_a.wait()
    place_a[...] = jnp.zeros_like(place_a)
    place_a[:n_i, :width_a] = a_in[...]
    a_parts[col] = pltpu.roll(place_a[...], lax.rem(col, 128 // width_a) * width_a, 1)
    got_target.wait()

    @pl.when(core == 0)
    def _():
        pl.semaphore_wait(barrier, n_rows - 1)
        pl.semaphore_signal(ok_sem, inc=1, device_id=(row + 1, col), device_id_type=MESH)

    @pl.when(core == 1)
    def _():
        pl.semaphore_wait(ok_sem, 1)

    sent_b = over_rows(b_parts.at[row], b_parts.at[row])
    sent_target = [send(stage.at[:, lanes(there)], target.at[row], there, col) for there in to_rows]
    got_c.wait()

    @pl.when(core == 1)
    def _():
        pl.semaphore_wait(barrier, 2 * (n_cols - 1))
        pl.semaphore_signal(ok_sem, inc=1, device_id=(row - 1, col), device_id_type=MESH)

    @pl.when(core == 0)
    def _():
        pl.semaphore_wait(ok_sem, 1)

    sent_a = over_cols(a_parts.at[col], a_parts.at[col])
    sent_c = share(c_whole, 0, col, over_cols)
    c_shard = c_whole[0, col]
    arrived(sent_b)
    b_full = widen(b_parts, width_b)
    arrived(sent_a)
    a_own = widen(a_parts, width_a)
    a_rows[0, row] = a_own
    sent_rows = share(a_rows, 0, row, over_rows)
    blocks = [row] + of_rows

    for step in range(STEPS):
        last = step == STEPS - 1
        term = {"c": None, "b": None, "own": None}
        sent_terms = [None] * (n_rows - 1)

        def add(name, value):
            term[name] = value if term[name] is None else term[name] + value

        def build(number):
            block = blocks[number]
            a_block = a_rows[step, block]
            for i in range(n_i):
                hi, lo = split(a_block[i : i + 1, :] * b_full)
                khatri_hi[block, i * n_j : (i + 1) * n_j, :] = hi
                khatri_lo[block, i * n_j : (i + 1) * n_j, :] = lo

        def probability(number):
            block = blocks[number]
            both = dot(khatri_hi[block], c_tall, ((1,), (1,)))
            model = both[:, :depth] + (both[:, depth:] + dot(khatri_lo[block], c_hi, ((1,), (1,))))
            return jax.nn.sigmoid(model)

        def derive(number, prob):
            block = blocks[number]
            hi, lo = split(prob - target[block])
            deriv[block, :, :depth] = hi
            deriv[block, :, depth:] = lo

        def third(number):
            block = blocks[number]
            both = dot(deriv[block], khatri_hi[block], ((0,), (0,)))
            cross = dot(deriv[block, :, :depth], khatri_lo[block], ((0,), (0,)))
            add("c", both[:depth] + (both[depth:] + cross))

        def others(number):
            block = blocks[number]
            deriv_c = dot(deriv[block], c_twice, ((1,), (0,)))
            deriv_c = deriv_c + dot(deriv[block, :, :depth], c_lo, ((1,), (0,)))
            deriv_c = deriv_c.reshape(n_i, n_j, rank)
            term_a = jnp.sum(deriv_c * b_full[None, :, :], axis=1)
            if number:
                a_leave[step, number - 1] = jnp.zeros_like(a_own)
                a_leave[step, number - 1, :n_i, :] = term_a
            else:
                term["own"] = term_a
            a_block = a_rows[step, block][:n_i, :]
            add("b", jnp.sum(deriv_c * a_block[:, None, :], axis=0))

        def deliver(number):
            sent_terms[number - 1] = send(
                a_leave.at[step, number - 1], a_arrive.at[step, number - 1], blocks[number], col
            )

        near, far = [0, 1], list(range(2, n_rows))
        build(0)
        if step == 0:
            arrived(sent_c)
        else:
            arrived(sent_rows)
            for number in [1] + far:
                build(number)
            arrived(sent_c)
        c_hi, c_lo = split(c_whole[step].reshape(-1, rank))
        c_tall = jnp.concatenate([c_hi, c_lo], axis=0)
        c_twice = jnp.concatenate([c_hi, c_hi], axis=0)
        if step == 0:
            prob = probability(0)
            got_own.wait()
            derive(0, prob)
            third(0)
            others(0)
            sent_rows[0].wait_recv()
            build(1)
            prob = probability(1)
            sent_target[0].wait_recv()
            derive(1, prob)
            third(1)
            others(1)
            deliver(1)
            arrived(sent_rows[1:])
            probs = []
            for number in far:
                build(number)
                probs.append(probability(number))
            arrived(sent_target[1:])
            for number, prob in zip(far, probs):
                derive(number, prob)
            for number in far:
                others(number)
            for number in far:
                deliver(number)
            for number in far:
                third(number)
        else:
            for number in far + near:
                derive(number, probability(number))
            for number in far:
                others(number)
            for number in far:
                deliver(number)
            for number in far + near:
                third(number)
        c_leave[step] = term["c"].reshape(c_leave.shape[1:])
        sent_c = [
            send(c_leave.at[step, there], c_arrive.at[step, k], row, there)
            for k, there in enumerate(to_cols)
        ]
        if step:
            others(1)
            deliver(1)
            others(0)
        b_slots[step, row] = term["b"]
        sent_b = share(b_slots, step, row, over_rows)
        a_leave[step, n_rows - 1] = jnp.zeros_like(a_own)
        a_leave[step, n_rows - 1, :n_i, :] = term["own"]
        arrived(sent_terms)
        term_own = a_leave[step, n_rows - 1]
        for k in range(n_rows - 1):
            term_own = term_own + a_arrive[step, k]
        a_slots[step, col] = term_own
        sent_a = share(a_slots, step, col, over_cols)
        arrived(sent_c)
        grad_c = c_leave[step, col]
        for k in range(n_cols - 1):
            grad_c = grad_c + c_arrive[step, k]
        c_shard = c_shard - rate[2] * grad_c
        if last:
            c_out[...] = c_shard
        else:
            c_whole[step + 1, col] = c_shard
            sent_c = share(c_whole, step + 1, col, over_cols)
        arrived(sent_b)
        b_full = b_full - rate[1] * total(b_slots, step)
        arrived(sent_a)
        a_own = a_own - rate[0] * total(a_slots, step)
        if not last:
            a_rows[step + 1, row] = a_own
            sent_rows = share(a_rows, step + 1, row, over_rows)
    back = lax.rem(n_cols - col, n_cols) * width_a
    a_out[...] = pltpu.roll(a_own, back, 1)[:n_i, :width_a]
    back = lax.rem(n_rows - row, n_rows) * width_b
    b_out[...] = pltpu.roll(b_full, back, 1)[:, :width_b]
    for copy in used:
        copy.wait_send()


def write_kernel(a_ref, b_ref, c_ref, a_out, b_out, c_out, sems):
    copies = [
        pltpu.make_async_copy(src, dst, sems.at[k])
        for k, (src, dst) in enumerate(((a_ref, a_out), (b_ref, b_out), (c_ref, c_out)))
    ]
    for copy in copies:
        copy.start()
    for copy in copies:
        copy.wait()


def n_copies(n_rows, n_cols):
    rows, cols = n_rows - 1, n_cols - 1
    return rows + (STEPS + 1) * (cols + rows) + STEPS * (rows + cols) + STEPS * (rows + cols)


def per_device(tensor, first_factor, second_factor, third_factor):
    n_rows, n_cols = lax.axis_size("rows"), lax.axis_size("cols")
    count, rank = third_factor.shape
    n_i, n_j, depth = tensor.shape
    part = depth // n_rows
    width_a, width_b = first_factor.shape[1], second_factor.shape[1]
    uneven = rank % 128 or width_a > 128 or 128 % width_a or width_b > 128 or 128 % width_b
    if count % 8 or n_rows % 2 or n_rows < 4 or n_j % 16 or part != 128 or uneven:
        return plain_steps(tensor, first_factor, second_factor, third_factor)
    tall = -(-n_i // 8) * 8
    f32, bf16 = jnp.float32, jnp.bfloat16
    copies = n_copies(n_rows, n_cols)
    vmem = pl.BlockSpec(memory_space=pltpu.VMEM)
    hbm = pl.BlockSpec(memory_space=pl.ANY)
    shapes = tuple(
        jax.ShapeDtypeStruct(x.shape, f32) for x in (first_factor, second_factor, third_factor)
    )
    results = pl.pallas_call(
        functools.partial(kernel, n_rows, n_cols, rates(tensor)),
        out_shape=shapes,
        in_specs=[hbm] * 4,
        out_specs=(vmem,) * 3,
        scratch_shapes=[
            pltpu.VMEM((n_i * n_j, depth), f32),
            pltpu.VMEM((n_rows, n_i * n_j, part), f32),
            pltpu.VMEM((n_i, width_a), f32),
            pltpu.VMEM((n_j, width_b), f32),
            pltpu.VMEM((n_cols, tall, 128), f32),
            pltpu.VMEM((n_rows, n_j, 128), f32),
            pltpu.VMEM((STEPS, n_cols, tall, rank), f32),
            pltpu.VMEM((STEPS, n_rows, tall, rank), f32),
            pltpu.VMEM((STEPS, n_rows, tall, rank), f32),
            pltpu.VMEM((STEPS, n_rows - 1, tall, rank), f32),
            pltpu.VMEM((STEPS, n_rows, n_j, rank), f32),
            pltpu.VMEM((STEPS, n_cols, count, rank), f32),
            pltpu.VMEM((STEPS, n_cols, count, rank), f32),
            pltpu.VMEM((STEPS, n_cols - 1, count, rank), f32),
            pltpu.VMEM((n_rows, n_i * n_j, rank), bf16),
            pltpu.VMEM((n_rows, n_i * n_j, rank), bf16),
            pltpu.VMEM((n_rows, n_i * n_j, 2 * part), bf16),
            pltpu.VMEM((tall, 128), f32),
            pltpu.VMEM((n_j, 128), f32),
            pltpu.SemaphoreType.DMA((5,)),
            pltpu.SemaphoreType.REGULAR,
            pltpu.SemaphoreType.DMA((copies,)),
            pltpu.SemaphoreType.DMA((copies,)),
        ],
        compiler_params=pltpu.CompilerParams(
            collective_id=0, has_side_effects=True, vmem_limit_bytes=VMEM_LIMIT
        ),
    )(tensor.reshape(n_i * n_j, depth), first_factor, second_factor, third_factor)
    return pl.pallas_call(
        write_kernel,
        out_shape=shapes,
        in_specs=[vmem] * 3,
        out_specs=(hbm,) * 3,
        scratch_shapes=[pltpu.SemaphoreType.DMA((3,))],
    )(*results)


def solution(mesh):
    in_specs = (
        P("rows", "cols", None),
        P("rows", "cols"),
        P("cols", "rows"),
        P(("rows", "cols"), None),
    )
    out_specs = (P("rows", "cols"), P("cols", "rows"), P(("rows", "cols"), None))
    return jax.shard_map(
        per_device, mesh=mesh, in_specs=in_specs, out_specs=out_specs, check_vma=False
    )
```

time: 49.7 us -> 43 us (0.87)
  local copies, waits for them, and re-layouts: 5.07 us -> 0 us
  Pallas kernels: 43.6 us -> 42 us
    unnamed x11 -> x0, local copies, waits for them, and re-layouts: 5.07 us -> none
    pallas_call x1, Pallas kernels: 43.6 us -> 40.7 us  [per_device(): pl.pallas_call(functools.partial(kernel, n_rows, n_cols, rates(tensor)),...]
    pallas_call x0 -> x1, Pallas kernels: none -> 1.39 us  [per_device(): pl.pallas_call(write_kernel, out_shape=shapes, in_specs=[vmem] * 3, out_s...]
where the time goes in v1:
time: 43 us; the launch traced here: 42.7 us
  Pallas kernels  42 us (98%)
  between operations  0.64 us (1%)
    pallas_call x1, Pallas kernels, per_device(): pl.pallas_call(functools.partial(kernel, n_rows, n_cols, rates(tensor)),...  40.7 us
    pallas_call x1, Pallas kernels, per_device(): pl.pallas_call(write_kernel, out_shape=shapes, in_specs=[vmem] * 3, out_s...  1.39 us

profile of v1, /device:TPU:0, one launch (start us, length us, event | category | flops | bytes accessed | tf_op | source)
XLA Modules:
  0.0 42.7 jit_solution(4437997007513780960)
XLA Ops:
  0.6 40.7 %shard_map.67 = (f32[12,32]{1,0:T(8,128)}, f32[32,64]{1,0:T(8,128)}, f32[16,256]{1,0:T(8,128)}) custom-call(f32[384,512]{1,0:T(8,128)} %bitcast.1, f32[12,32]{1,0:T(8,128)} %a_hbm.1, f32[32,64]{1,0:T(8,128)} %b_hbm.1, f32[16,256]{1,0:T(8,128)} %c_hbm.1), custom_call_target="tpu_custom_call" | custom-call | tf_op jit(solution)/shard_map/pallas_call | solution.py:389
  41.3 1.4 %shard_map.68 = (f32[12,32]{1,0:T(8,128)}, f32[32,64]{1,0:T(8,128)}, f32[16,256]{1,0:T(8,128)}) custom-call(f32[12,32]{1,0:T(8,128)} %get-tuple-element.6.a_ref, f32[32,64]{1,0:T(8,128)} %get-tuple-element.7.b_ref, f32[16,256]{1,0:T(8,128)} %get-tuple-element.8.c_ref), custom_call_target="tpu_custom_call" | custom-call | tf_op jit(solution)/shard_map/pallas_call | solution.py:423

commit v2 on v1

--- a/solution.py
+++ b/solution.py
@@ -8,7 +8,7 @@
 from jax.sharding import PartitionSpec as P
 
 STEPS = 2
-VMEM_LIMIT = 67043328
+VMEM_LIMIT = 48 << 20
 MESH = pl.DeviceIdType.MESH
 
 
@@ -84,7 +84,7 @@
     depth = target.shape[2]
     row, col = lax.axis_index("rows"), lax.axis_index("cols")
     plane, core = lax.div(row, 2), lax.rem(row, 2)
-    used, loads = [], []
+    used, loads, gone = [], [], set()
 
     def turn(base, offset, size):
         return lax.rem(base + offset, size)
@@ -105,13 +105,21 @@
         copy.start()
         return copy
 
+    def flipped(place, mask):
+        for bit in (1 << k for k in range(mask.bit_length()) if mask >> k & 1):
+            place = place + bit - 2 * bit * lax.rem(lax.div(place, bit), 2)
+        return place
+
     steps_away = [(h, flip) for h in range(half) for flip in (0, 1)][1:]
     to_rows = [turn(plane, h, half) * 2 + lax.rem(core + flip, 2) for h, flip in steps_away]
     of_rows = [turn(plane, half - h, half) * 2 + lax.rem(core + flip, 2) for h, flip in steps_away]
-    to_cols = [turn(col, k, n_cols) for k in range(1, n_cols)]
+    to_cols = [flipped(col, mask) for mask in reversed(range(1, n_cols))]
 
     def lanes(block):
         return pl.ds(pl.multiple_of(block * depth, 128), depth)
+
+    def tile(there):
+        return pl.ds(pl.multiple_of(lax.div(there * width_a, 128) * 128, 128), 128)
 
     def greet(there_row, there_col):
         pl.semaphore_signal(
@@ -130,10 +138,18 @@
         greet(plane * 2 + 1, there)
 
     got_b = load(b_hbm, b_in)
-    got_target = load(target_hbm, stage)
+    got_target = [
+        load(target_hbm.at[:, lanes(there)], stage.at[k]) for k, there in enumerate(to_rows)
+    ]
     got_a = load(a_hbm, a_in)
     got_c = load(c_hbm, c_whole.at[0, col])
     got_own = load(target_hbm.at[:, lanes(row)], target.at[row])
+
+    def left(copies):
+        for copy in copies:
+            if id(copy) not in gone:
+                gone.add(id(copy))
+                copy.wait_send()
 
     def over_cols(src, dst):
         return [send(src, dst, row, there) for there in to_cols]
@@ -172,7 +188,8 @@
     place_a[...] = jnp.zeros_like(place_a)
     place_a[:n_i, :width_a] = a_in[...]
     a_parts[col] = pltpu.roll(place_a[...], lax.rem(col, 128 // width_a) * width_a, 1)
-    got_target.wait()
+    for copy in got_target:
+        copy.wait()
 
     @pl.when(core == 0)
     def _():
@@ -184,7 +201,16 @@
         pl.semaphore_wait(ok_sem, 1)
 
     sent_b = over_rows(b_parts.at[row], b_parts.at[row])
-    sent_target = [send(stage.at[:, lanes(there)], target.at[row], there, col) for there in to_rows]
+    sent_target = [
+        send(stage.at[k], target.at[row], there, col) for k, there in enumerate(to_rows[:-1])
+    ]
+    rows_dev = n_i * n_j
+    early = rows_dev * 3 // 4 // 8 * 8
+    sent_target.append(
+        send(
+            stage.at[n_rows - 2, :early], target.at[row, :early], to_rows[-1], col
+        )
+    )
     got_c.wait()
 
     @pl.when(core == 1)
@@ -205,6 +231,11 @@
     a_own = widen(a_parts, width_a)
     a_rows[0, row] = a_own
     sent_rows = share(a_rows, 0, row, over_rows)
+    sent_target.append(
+        send(
+            stage.at[n_rows - 2, early:], target.at[row, early:], to_rows[-1], col
+        )
+    )
     blocks = [row] + of_rows
 
     for step in range(STEPS):
@@ -327,7 +358,17 @@
         for k in range(n_rows - 1):
             term_own = term_own + a_arrive[step, k]
         a_slots[step, col] = term_own
-        sent_a = share(a_slots, step, col, over_cols)
+        if last:
+            sent_a = [
+                send(
+                    a_slots.at[step, col, :, tile(there)], a_slots.at[step, col, :, tile(there)],
+                    row, there,
+                )
+                for there in to_cols
+            ]
+        else:
+            sent_a = share(a_slots, step, col, over_cols)
+        left(used if last else used[: -n_cols + 1])
         arrived(sent_c)
         grad_c = c_leave[step, col]
         for k in range(n_cols - 1):
@@ -341,16 +382,20 @@
         arrived(sent_b)
         b_full = b_full - rate[1] * total(b_slots, step)
         arrived(sent_a)
-        a_own = a_own - rate[0] * total(a_slots, step)
         if not last:
+            a_own = a_own - rate[0] * total(a_slots, step)
             a_rows[step + 1, row] = a_own
             sent_rows = share(a_rows, step + 1, row, over_rows)
-    back = lax.rem(n_cols - col, n_cols) * width_a
+    grad_a = a_slots[STEPS - 1, 0, :, tile(col)]
+    for k in range(1, n_cols):
+        grad_a = grad_a + a_slots[STEPS - 1, k, :, tile(col)]
+    a_own = a_rows[STEPS - 1, row, :, tile(col)] - rate[0] * grad_a
+    per = 128 // width_a
+    back = lax.rem(per - lax.rem(col, per), per) * width_a
     a_out[...] = pltpu.roll(a_own, back, 1)[:n_i, :width_a]
     back = lax.rem(n_rows - row, n_rows) * width_b
     b_out[...] = pltpu.roll(b_full, back, 1)[:, :width_b]
-    for copy in used:
-        copy.wait_send()
+    left(used)
 
 
 def write_kernel(a_ref, b_ref, c_ref, a_out, b_out, c_out, sems):
@@ -366,7 +411,7 @@
 
 def n_copies(n_rows, n_cols):
     rows, cols = n_rows - 1, n_cols - 1
-    return rows + (STEPS + 1) * (cols + rows) + STEPS * (rows + cols) + STEPS * (rows + cols)
+    return 1 + rows + (STEPS + 1) * (cols + rows) + STEPS * (rows + cols) + STEPS * (rows + cols)
 
 
 def per_device(tensor, first_factor, second_factor, third_factor):
@@ -376,7 +421,7 @@
     part = depth // n_rows
     width_a, width_b = first_factor.shape[1], second_factor.shape[1]
     uneven = rank % 128 or width_a > 128 or 128 % width_a or width_b > 128 or 128 % width_b
-    if count % 8 or n_rows % 2 or n_rows < 4 or n_j % 16 or part != 128 or uneven:
+    if count % 8 or n_rows % 2 or n_rows < 4 or n_cols & (n_cols - 1) or n_j % 16 or part != 128 or uneven:
         return plain_steps(tensor, first_factor, second_factor, third_factor)
     tall = -(-n_i // 8) * 8
     f32, bf16 = jnp.float32, jnp.bfloat16
@@ -392,7 +437,7 @@
         in_specs=[hbm] * 4,
         out_specs=(vmem,) * 3,
         scratch_shapes=[
-            pltpu.VMEM((n_i * n_j, depth), f32),
+            pltpu.VMEM((n_rows - 1, n_i * n_j, part), f32),
             pltpu.VMEM((n_rows, n_i * n_j, part), f32),
             pltpu.VMEM((n_i, width_a), f32),
             pltpu.VMEM((n_j, width_b), f32),
@@ -411,7 +456,7 @@
             pltpu.VMEM((n_rows, n_i * n_j, 2 * part), bf16),
             pltpu.VMEM((tall, 128), f32),
             pltpu.VMEM((n_j, 128), f32),
-            pltpu.SemaphoreType.DMA((5,)),
+            pltpu.SemaphoreType.DMA((n_rows + 3,)),
             pltpu.SemaphoreType.REGULAR,
             pltpu.SemaphoreType.DMA((copies,)),
             pltpu.SemaphoreType.DMA((copies,)),
@@ -419,13 +464,14 @@
         compiler_params=pltpu.CompilerParams(
             collective_id=0, has_side_effects=True, vmem_limit_bytes=VMEM_LIMIT
         ),
-    )(tensor.reshape(n_i * n_j, depth), first_factor, second_factor, third_factor)
+    )(*[pltpu.with_memory_space_constraint(x, pltpu.HBM) for x in (tensor.reshape(n_i * n_j, depth), first_factor, second_factor, third_factor)])
     return pl.pallas_call(
         write_kernel,
         out_shape=shapes,
         in_specs=[vmem] * 3,
         out_specs=(hbm,) * 3,
         scratch_shapes=[pltpu.SemaphoreType.DMA((3,))],
+        compiler_params=pltpu.CompilerParams(vmem_limit_bytes=1 << 20),
     )(*results)
 
 

time: 43 us -> 40.6 us (0.944)
  Pallas kernels: 42 us -> 39.7 us
    pallas_call x1, Pallas kernels: 40.7 us -> 39 us  [per_device(): pl.pallas_call(functools.partial(kernel, n_rows, n_cols, rates(tensor)),...]
    pallas_call x1, Pallas kernels: 1.39 us -> 0.64 us  [per_device(): pl.pallas_call(write_kernel, out_shape=shapes, in_specs=[vmem] * 3, out_s...]
where the time goes in v2:
time: 40.6 us; the launch traced here: 40.3 us
  Pallas kernels  39.7 us (98%)
  between operations  0.64 us (2%)
    pallas_call x1, Pallas kernels, per_device(): pl.pallas_call(functools.partial(kernel, n_rows, n_cols, rates(tensor)),...  39 us

profile of v2, /device:TPU:0, one launch (start us, length us, event | category | flops | bytes accessed | tf_op | source)
XLA Modules:
  0.0 40.3 jit_solution(8734482857818057970)
XLA Ops:
  0.6 39.0 %shard_map.67 = (f32[12,32]{1,0:T(8,128)S(1)}, f32[32,64]{1,0:T(8,128)S(1)}, f32[16,256]{1,0:T(8,128)S(1)}) custom-call(f32[384,512]{1,0:T(8,128)} %bitcast.1, f32[12,32]{1,0:T(8,128)} %a_hbm.1, f32[32,64]{1,0:T(8,128)} %b_hbm.1, f32[16,256]{1,0:T(8,128)} %c_hbm.1), custom_call_target="tpu_custom_call" | custom-call | tf_op jit(solution)/shard_map/pallas_call | solution.py:434
  39.7 0.6 %shard_map.68 = (f32[12,32]{1,0:T(8,128)}, f32[32,64]{1,0:T(8,128)}, f32[16,256]{1,0:T(8,128)}) custom-call(f32[12,32]{1,0:T(8,128)S(1)} %get-tuple-element.6.a_ref, f32[32,64]{1,0:T(8,128)S(1)} %get-tuple-element.7.b_ref, f32[16,256]{1,0:T(8,128)S(1)} %get-tuple-element.8.c_ref), custom_call_target="tpu_custom_call" | custom-call | tf_op jit(solution)/shard_map/pallas_call | solution.py:468
